TPU v7x, 32 devices: a whole 2x2x4 slice. The times are simulated.
32 devices in a mesh: shots: 2 (over x), gx: 16 (over z, y, core).
Axes of the slice: x: 2, y: 2, z: 4, core: 2. Of those that a mesh axis runs over, the one named last changes fastest.
Arguments:
- velocity: float32 [256, 24, 128], P('gx'), may hold values from 0.05 to 0.18
- source_prior: float32 [512, 24, 128], P(('shots', 'gx')), parts along dimension 0, may hold values from -6 to 6
- source_now: float32 [512, 24, 128], P(('shots', 'gx')), parts along dimension 0, may hold values from -6 to 6
- record_prior: float32 [512, 24, 128], P(('shots', 'gx')), parts along dimension 0, may hold values from -6 to 6
- record_now: float32 [512, 24, 128], P(('shots', 'gx')), parts along dimension 0, may hold values from -6 to 6
- source_inline: int32 [32], P('shots'), parts along dimension 0, may hold values from 0 to 255
- source_crossline: int32 [32], P('shots'), parts along dimension 0, may hold values from 0 to 23
- source_pulse: float32 [32, 2], P('shots'), parts along dimension 0, may hold values from -12 to 12
- receiver_inline: int32 [2048], P('shots'), parts along dimension 0, may hold values from 0 to 255
- receiver_crossline: int32 [2048], P('shots'), parts along dimension 0, may hold values from 0 to 23
- receiver_trace: float32 [2048, 2], P('shots'), parts along dimension 0, may hold values from -12 to 12
- offsets: int32 [17], replicated, may hold values from -8 to 8
Outputs:
- images: bfloat16 [34, 256, 24, 128], P('shots', 'gx'), parts along dimension 0
- adjoint_source: float32 [512, 24, 128], P(('shots', 'gx')), parts along dimension 0
- adjoint_receiver: float32 [512, 24, 128], P(('shots', 'gx')), parts along dimension 0
There are 2 independent parts, one for each index of `shots`. A program takes and returns all parts, laid end to end along the dimension named above; an argument that names none is the same for every part. Nothing has to cross between parts.
All inputs are finite; a program needn't handle non-finite values.
Results may differ from a plain program's by a relative error of at most 0.001.
Values sent between devices are 32-bit elements; how exact they have to be, the bound alone decides.
No kernel may reach another device: no remote copies, remote signals or barrier semaphores. Data moves between devices by JAX's collectives and lax.ppermute only.
A program may use at most 128 MiB of HBM per device.

v0:
```python
import jax
import jax.numpy as jnp
from jax import lax
from jax.sharding import PartitionSpec as P

STEPS = 2
NLAG = 17
LAG_MAX = 8


stencil = (-205.0 / 72.0, 8.0 / 5.0, -1.0 / 5.0, 8.0 / 315.0, -1.0 / 560.0)
source_depth = 3
record_depth = 1


def extended(shard, sides, width):
    for axis, dim in sides:
        count, length = (lax.axis_size(axis), shard.shape[dim])
        up = [(i, (i + 1) % count) for i in range(count - 1)]
        down = [(j, i) for i, j in up]
        last = lax.slice_in_dim(shard, length - width, length, axis=dim)
        first = lax.slice_in_dim(shard, 0, width, axis=dim)
        before = lax.ppermute(last, axis, up)
        after = lax.ppermute(first, axis, down)
        shard = jnp.concatenate([before, shard, after], axis=dim)
    return shard


def from_behind(block, axis, distance):
    devices = range(lax.axis_size(axis))
    route = [(i - distance, i) for i in devices if i - distance in devices]
    return lax.ppermute(block, axis, route)


def laplace_trim(wide):
    length = wide.shape[1] - 8
    cells_y = wide.shape[2]
    cells_z = wide.shape[3]
    padded = jnp.pad(wide, ((0, 0), (0, 0), (4, 4), (4, 4)))
    summed = 3.0 * stencil[0] * padded[:, 4 : 4 + length, 4 : 4 + cells_y, 4 : 4 + cells_z]
    for offset in range(1, 5):
        beside_all = padded[:, 4 + offset : 4 + offset + length, 4 : 4 + cells_y, 4 : 4 + cells_z]
        beside_all = (
            beside_all
            + padded[:, 4 - offset : 4 - offset + length, 4 : 4 + cells_y, 4 : 4 + cells_z]
        )
        beside_all = (
            beside_all
            + padded[:, 4 : 4 + length, 4 + offset : 4 + offset + cells_y, 4 : 4 + cells_z]
        )
        beside_all = (
            beside_all
            + padded[:, 4 : 4 + length, 4 - offset : 4 - offset + cells_y, 4 : 4 + cells_z]
        )
        beside_all = (
            beside_all
            + padded[:, 4 : 4 + length, 4 : 4 + cells_y, 4 + offset : 4 + offset + cells_z]
        )
        beside_all = (
            beside_all
            + padded[:, 4 : 4 + length, 4 : 4 + cells_y, 4 - offset : 4 - offset + cells_z]
        )
        summed = summed + stencil[offset] * beside_all
    return summed


def injection(place_x, place_y, amplitude, anchor, count_x, count_y):
    hits_x = (place_x[:, None] - anchor == jnp.arange(count_x, dtype=jnp.int32)[None, :]).astype(
        jnp.float32
    ) * amplitude[:, None]
    hits_y = (place_y[:, None] == jnp.arange(count_y, dtype=jnp.int32)[None, :]).astype(jnp.float32)
    return jnp.einsum("sx,sy->xy", hits_x, hits_y, precision=lax.Precision.HIGHEST)


def accumulate_terms(squares, offsets, length):
    weights = (offsets * offsets).astype(jnp.float32) / (LAG_MAX * LAG_MAX * NLAG)

    def accumulate(index, carry):
        shift_cells = offsets[index]
        from_record = lax.dynamic_slice_in_dim(squares[1], 2 * LAG_MAX + 2 * shift_cells, length, 0)
        from_source = lax.dynamic_slice_in_dim(squares[0], 2 * LAG_MAX - 2 * shift_cells, length, 0)
        return carry + weights[index] * jnp.stack([from_record, from_source])

    empty = jnp.zeros((2, length) + squares.shape[2:], jnp.float32)
    return lax.fori_loop(0, NLAG, accumulate, empty)


def image_stack(wide, reach, offsets, extent):

    def single(shift_cells):
        left = lax.dynamic_slice_in_dim(wide[0], reach - shift_cells, extent, 0)
        right = lax.dynamic_slice_in_dim(wide[1], reach + shift_cells, extent, 0)
        return (left * right).astype(jnp.bfloat16)

    return jax.vmap(single)(offsets)


def per_device(
    velocity,
    source_prior,
    source_now,
    record_prior,
    record_now,
    source_inline,
    source_crossline,
    source_pulse,
    receiver_inline,
    receiver_crossline,
    receiver_trace,
    offsets,
):
    extent = velocity.shape[0]
    cells_y = velocity.shape[1]
    anchor = lax.axis_index("gx") * extent
    current = jnp.stack([source_now, record_now])
    previous = jnp.stack([source_prior, record_prior])
    for moment in range(STEPS):
        wide = extended(current, (("gx", 1),), 4)
        upcoming = 2.0 * current - previous + velocity[None] * laplace_trim(wide)
        field = upcoming
        source_plane = injection(
            source_inline, source_crossline, source_pulse[:, moment], anchor, extent, cells_y
        )
        record_plane = injection(
            receiver_inline, receiver_crossline, receiver_trace[:, moment], anchor, extent, cells_y
        )
        field = field.at[0, :, :, source_depth].add(source_plane)
        upcoming = field.at[1, :, :, record_depth].add(record_plane)
        previous, current = (current, upcoming)
    wide = extended(current, (("gx", 1),), LAG_MAX)
    images = image_stack(wide, LAG_MAX, offsets, extent)
    squares = jnp.pad(current * current, ((0, 0), (4 * LAG_MAX, 4 * LAG_MAX), (0, 0), (0, 0)))
    terms = accumulate_terms(squares, offsets, extent + 4 * LAG_MAX)
    lower_rim = terms[:, : 2 * LAG_MAX]
    upper_rim = terms[:, extent + 2 * LAG_MAX :]
    middle = terms[:, 2 * LAG_MAX : 2 * LAG_MAX + extent]
    from_lower = from_behind(upper_rim, "gx", 1)
    from_upper = from_behind(lower_rim, "gx", -1)
    middle = middle.at[:, : 2 * LAG_MAX].add(from_lower)
    middle = middle.at[:, extent - 2 * LAG_MAX :].add(from_upper)
    return (images, current[0] * middle[0], current[1] * middle[1])


def solution(mesh):
    in_specs = (
        P("gx", None, None),
        P(("shots", "gx"), None, None),
        P(("shots", "gx"), None, None),
        P(("shots", "gx"), None, None),
        P(("shots", "gx"), None, None),
        P("shots"),
        P("shots"),
        P("shots", None),
        P("shots"),
        P("shots"),
        P("shots", None),
        P(),
    )
    out_specs = (
        P("shots", "gx", None, None),
        P(("shots", "gx"), None, None),
        P(("shots", "gx"), None, None),
    )
    return jax.shard_map(
        per_device, mesh=mesh, in_specs=in_specs, out_specs=out_specs, check_vma=False
    )
```

profile of v0, /device:TPU:10, one launch (start us, length us, event | category | flops | bytes accessed | tf_op | source)
XLA Modules:
  0.0 124.2 jit_solution(5781560303846381513)
XLA Ops:
  0.7 1.0 fusion.59
  1.6 1.9 %collective-permute-start.1 = (f32[2,4,24,128]{3,2,1,0:T(8,128)S(1)}, f32[2,4,24,128]{3,2,1,0:T(8,128)S(1)}, u32[]{:S(2)}, u32[]{:S(2)}) collective-permute-start(f32[2,4,24,128]{3,2,1,0:T(8,128)S(1)} %get-tuple-element.308), channel_id=1, source_target_pairs={{0,1},{1,2},{2,3},{3,4},{4,5},{5,6},{6,7},{7,8},{8,9},{9,10},{10,1... | collective-permute-start | bytes 294920 | tf_op jit(solution)/shard_map/ppermute | solution.py:23
  3.6 4.5 %collective-permute-start = (f32[2,4,24,128]{3,2,1,0:T(8,128)S(1)}, f32[2,4,24,128]{3,2,1,0:T(8,128)S(1)}, u32[]{:S(2)}, u32[]{:S(2)}) collective-permute-start(f32[2,4,24,128]{3,2,1,0:T(8,128)S(1)} %get-tuple-element.309), channel_id=1, source_target_pairs={{1,0},{2,1},{3,2},{4,3},{5,4},{6,5},{7,6},{8,7},{9,8},{10,9},{11,1... | collective-permute-start | bytes 294920 | tf_op jit(solution)/shard_map/ppermute | solution.py:24
  8.1 1.2 convert_multiply_fusion
  9.3 0.7 fusion.72
  10.6 0.8 slice_bitcast_fusion.2
  11.3 0.7 broadcast_subtract_fusion.1
  12.0 0.7 broadcast_subtract_fusion
  12.7 0.8 fusion.82
  13.5 1.7 %convolution_bitcast_fusion.2 = f32[1,16,24,1]{2,1,3,0:T(8,128)S(1)} fusion(s32[1024]{0:T(1024)} %param.39, f32[1024]{0:T(1024)S(1)} %bitcast.56, s32[1024]{0:T(1024)S(1)} %broadcast_subtract_fusion), kind=kOutput, calls=%fused_computation.21 | convolution fusion | flops 4775936 | bytes 13824 | tf_op jit(solution)/shard_map/sx,sy->xy/dot_general | solution.py:72
  15.2 1.7 %convolution_bitcast_fusion = f32[1,16,24,1]{2,1,3,0:T(8,128)S(1)} fusion(f32[1024]{0:T(1024)S(1)} %bitcast.55, s32[1024]{0:T(1024)} %param.39, s32[1024]{0:T(1024)S(1)} %broadcast_subtract_fusion), kind=kOutput, calls=%fused_computation.19 | convolution fusion | flops 4775936 | bytes 13824 | tf_op jit(solution)/shard_map/sx,sy->xy/dot_general | solution.py:72
  17.7 2.0 %and_reduce_fusion = pred[]{:T(512)} fusion(s32[4]{0:T(128)S(1)} %copy-done.5, s32[1]{0:T(128)} %get-tuple-element.316, s32[1]{0:T(128)} %constant.273.clone.1, s32[1]{0:T(128)} %get-tuple-element.317), kind=kLoop, calls=%fused_computation.152 | loop fusion | flops 27 | bytes 29 | tf_op jit(solution)/shard_map/reduce.6
  20.8 1.6 %fusion.41 = f32[2,16,24,128]{3,2,1,0:T(8,128)S(1)} fusion(f32[2,24,32,136]{3,2,1,0:T(8,128)S(1)} %select_maximum_fusion.2, f32[2,20,24,128]{3,2,1,0:T(8,128)S(1)} %get-tuple-element.307, f32[2,20,24,128]{3,2,1,0:T(8,128)S(1)} %get-tuple-element.306, f32[1,16,24,128]{3,2,1,0:T(8,128)S(1)} %bitcast.53, f32[1,16,24,128]{3,2,1,0:T(8,128)S(1)} %bitcast.54, ...), kind=kLoop, calls=%fused_computation.91 | loop fusion | flops 3440640 | bytes 10813440 | tf_op jit(solution)/shard_map/add | solution.py:119
  22.4 2.1 %add_select_fusion.1 = f32[1,16,24,1]{3,2,1,0:T(8,128)S(1)} fusion(f32[1,16,24,1]{3,2,1,0:T(8,128)S(1)} %copy.90, f32[2,16,24,128]{3,2,1,0:T(8,128)S(1)} %fusion.41, s32[]{:T(128)} %bitcast.4, s32[]{:T(128)} %bitcast.5, pred[]{:T(512)} %and_reduce_fusion), kind=kLoop, calls=%fused_computation.120 | loop fusion | flops 768 | bytes 4617 | tf_op jit(solution)/shard_map/select.6
  24.5 2.6 %scatter-add.14 = f32[2,16,24,128]{3,2,1,0:T(8,128)S(1)} dynamic-update-slice(f32[2,16,24,128]{3,2,1,0:T(8,128)S(1)} %fusion.41, f32[1,16,24,1]{3,2,1,0:T(8,128)S(1)} %add_select_fusion.1, s32[]{:T(128)} %bitcast.4, s32[]{:T(128)} %constant.271.clone.1, s32[]{:T(128)} %constant.271.clone.1, s32[]{:T(128)} %bitcast.5) | dynamic-update-slice | bytes 3076 | tf_op jit(solution)/shard_map/scatter-add | solution.py:127
  27.2 1.3 %scatter-add.15 = f32[2,16,24,128]{3,2,1,0:T(8,128)S(1)} dynamic-update-slice(f32[2,16,24,128]{3,2,1,0:T(8,128)S(1)} %scatter-add.14, f32[1,16,24,1]{3,2,1,0:T(8,128)S(1)} %slice_add_fusion.25, s32[]{:T(128)} %constant.278.clone.1, s32[]{:T(128)} %constant.271.clone.1, s32[]{:T(128)} %constant.271.clone.1, s32[]{:T(128)} %constant.278.clone.1) | dynamic-update-slice | bytes 3076 | tf_op jit(solution)/shard_map/scatter-add | solution.py:128
  28.5 1.9 %collective-permute-start.2 = (f32[2,4,24,128]{3,2,1,0:T(8,128)S(1)}, f32[2,4,24,128]{3,2,1,0:T(8,128)S(1)}, u32[]{:S(2)}, u32[]{:S(2)}) collective-permute-start(f32[2,4,24,128]{3,2,1,0:T(8,128)S(1)} %get-tuple-element.304), channel_id=1, source_target_pairs={{1,0},{2,1},{3,2},{4,3},{5,4},{6,5},{7,6},{8,7},{9,8},{10,9},{11,1... | collective-permute-start | bytes 294920 | tf_op jit(solution)/shard_map/ppermute | solution.py:24
  30.5 2.4 %collective-permute-start.3 = (f32[2,4,24,128]{3,2,1,0:T(8,128)S(1)}, f32[2,4,24,128]{3,2,1,0:T(8,128)S(1)}, u32[]{:S(2)}, u32[]{:S(2)}) collective-permute-start(f32[2,4,24,128]{3,2,1,0:T(8,128)S(1)} %get-tuple-element.305), channel_id=1, source_target_pairs={{0,1},{1,2},{2,3},{3,4},{4,5},{5,6},{6,7},{7,8},{8,9},{9,10},{10,1... | collective-permute-start | bytes 294920 | tf_op jit(solution)/shard_map/ppermute | solution.py:23
  33.3 4.0 %collective-permute-done.3 = f32[2,4,24,128]{3,2,1,0:T(8,128)S(1)} collective-permute-done((f32[2,4,24,128]{3,2,1,0:T(8,128)S(1)}, f32[2,4,24,128]{3,2,1,0:T(8,128)S(1)}, u32[]{:S(2)}, u32[]{:S(2)}) %collective-permute-start.3) | collective-permute-done | bytes 98336 | tf_op jit(solution)/shard_map/ppermute | solution.py:23
  37.8 1.6 %fusion.16 = f32[2,16,24,128]{3,2,1,0:T(8,128)S(1)} fusion(f32[2,16,24,128]{3,2,1,0:T(8,128)S(1)} %scatter-add.15, f32[2,4,24,128]{3,2,1,0:T(8,128)S(1)} %collective-permute-done.3, f32[2,4,24,128]{3,2,1,0:T(8,128)S(1)} %collective-permute-done.2, f32[2,24,32,136]{3,2,1,0:T(8,128)S(1)} %select_maximum_fusion, f32[1,16,24,128]{3,2,1,0:T(8,128)S(1)} %bitcast.52, ...), kind=kLoop, calls=%fused_computation.57 | loop fusion | flops 4128768 | bytes 7864320 | tf_op jit(solution)/shard_map/add | solution.py:119
  39.4 2.1 %add_select_fusion = f32[1,16,24,1]{3,2,1,0:T(8,128)S(1)} fusion(f32[1,16,24,1]{3,2,1,0:T(8,128)S(1)} %copy.92, f32[2,16,24,128]{3,2,1,0:T(8,128)S(1)} %fusion.16, s32[]{:T(128)} %bitcast.4, s32[]{:T(128)} %bitcast.5, pred[]{:T(512)} %and_reduce_fusion), kind=kLoop, calls=%fused_computation.119 | loop fusion | flops 768 | bytes 4617 | tf_op jit(solution)/shard_map/select.8
  41.5 2.6 %scatter-add.16 = f32[2,16,24,128]{3,2,1,0:T(8,128)S(1)} dynamic-update-slice(f32[2,16,24,128]{3,2,1,0:T(8,128)S(1)} %fusion.16, f32[1,16,24,1]{3,2,1,0:T(8,128)S(1)} %add_select_fusion, s32[]{:T(128)} %bitcast.4, s32[]{:T(128)} %constant.271.clone.1, s32[]{:T(128)} %constant.271.clone.1, s32[]{:T(128)} %bitcast.5) | dynamic-update-slice | bytes 3076 | tf_op jit(solution)/shard_map/scatter-add | solution.py:127
  44.2 1.3 %scatter-add.19 = f32[2,16,24,128]{3,2,1,0:T(8,128)S(1)} dynamic-update-slice(f32[2,16,24,128]{3,2,1,0:T(8,128)S(1)} %scatter-add.16, f32[1,16,24,1]{3,2,1,0:T(8,128)S(1)} %slice_add_fusion.24, s32[]{:T(128)} %constant.278.clone.1, s32[]{:T(128)} %constant.271.clone.1, s32[]{:T(128)} %constant.271.clone.1, s32[]{:T(128)} %constant.278.clone.1) | dynamic-update-slice | bytes 3076 | tf_op jit(solution)/shard_map/scatter-add | solution.py:128
  45.6 0.8 fusion.80
  46.4 1.9 %collective-permute-start.4 = (f32[2,8,24,128]{3,2,1,0:T(8,128)}, f32[2,8,24,128]{3,2,1,0:T(8,128)}, u32[]{:S(2)}, u32[]{:S(2)}) collective-permute-start(f32[2,8,24,128]{3,2,1,0:T(8,128)} %get-tuple-element.302), channel_id=1, source_target_pairs={{0,1},{1,2},{2,3},{3,4},{4,5},{5,6},{6,7},{7,8},{8,9},{9,10},{10,1... | collective-permute-start | bytes 589832 | tf_op jit(solution)/shard_map/ppermute | solution.py:23
  48.3 4.5 %collective-permute-start.5 = (f32[2,8,24,128]{3,2,1,0:T(8,128)}, f32[2,8,24,128]{3,2,1,0:T(8,128)}, u32[]{:S(2)}, u32[]{:S(2)}) collective-permute-start(f32[2,8,24,128]{3,2,1,0:T(8,128)} %get-tuple-element.303), channel_id=1, source_target_pairs={{1,0},{2,1},{3,2},{4,3},{5,4},{6,5},{7,6},{8,7},{9,8},{10,9},{11,1... | collective-permute-start | bytes 589832 | tf_op jit(solution)/shard_map/ppermute | solution.py:24
  53.0 52.0 %while.25 = (s32[]{:T(128)}, f32[2,48,24,128]{3,2,1,0:T(8,128)S(1)}, f32[17]{0:T(128)S(1)}, f32[2,80,24,128]{3,2,1,0:T(8,128)S(1)}, s32[17]{0:T(128)S(1)}, /*ind...) while((s32[]{:T(128)}, f32[2,48,24,128]{3,2,1,0:T(8,128)S(1)}, ...), condition=%wide.region_2.3_spmd.clone, body=%wide.region_1.2_spmd.clone.sunk | while | flops 1179660 | bytes 9830659 | solution.py:85
  53.0 0.6 dynamic_slice.43
  55.1 0.9 fusion.87
  56.1 0.6 dynamic_slice.43
  58.1 0.9 fusion.87
  59.1 0.6 dynamic_slice.43
  61.2 0.9 fusion.87
  62.2 0.6 dynamic_slice.43
  64.3 0.9 fusion.87
  65.2 0.6 dynamic_slice.43
  67.3 0.9 fusion.87
  68.3 0.6 dynamic_slice.43
  70.4 0.9 fusion.87
  71.4 0.6 dynamic_slice.43
  73.5 0.9 fusion.87
  74.4 0.6 dynamic_slice.43
  76.5 0.9 fusion.87
  77.5 0.6 dynamic_slice.43
  79.6 0.9 fusion.87
  80.5 0.6 dynamic_slice.43
  82.6 0.9 fusion.87
  83.6 0.6 dynamic_slice.43
  85.7 0.9 fusion.87
  86.7 0.6 dynamic_slice.43
  88.8 0.9 fusion.87
  91.8 0.9 fusion.87
  94.9 0.9 fusion.87
  97.9 0.9 fusion.87
  101.0 0.9 fusion.87
  104.0 0.9 fusion.87
  105.0 0.8 fusion.79
  105.8 1.9 %collective-permute-start.6 = (f32[2,16,24,128]{3,2,1,0:T(8,128)}, f32[2,16,24,128]{3,2,1,0:T(8,128)S(1)}, u32[]{:S(2)}, u32[]{:S(2)}) collective-permute-start(f32[2,16,24,128]{3,2,1,0:T(8,128)} %get-tuple-element.296), channel_id=1, source_target_pairs={{0,1},{1,2},{2,3},{3,4},{4,5},{5,6},{6,7},{7,8},{8,9},{9,10},{10,1... | collective-permute-start | bytes 1179656 | tf_op jit(solution)/shard_map/ppermute | solution.py:32
  107.7 4.5 %collective-permute-start.7 = (f32[2,16,24,128]{3,2,1,0:T(8,128)S(1)}, f32[2,16,24,128]{3,2,1,0:T(8,128)S(1)}, u32[]{:S(2)}, u32[]{:S(2)}) collective-permute-start(f32[2,16,24,128]{3,2,1,0:T(8,128)S(1)} %get-tuple-element.297), channel_id=1, source_target_pairs={{1,0},{2,1},{3,2},{4,3},{5,4},{6,5},{7,6},{8,7},{9,8},{10,9},{11,1... | collective-permute-start | bytes 1179656 | tf_op jit(solution)/shard_map/ppermute | solution.py:32
  112.3 1.1 pad_maximum_fusion
  113.5 2.7 %gather_fusion.1 = f32[17,16,24,128]{3,2,1,0:T(8,128)} fusion(f32[32,24,128]{2,1,0:T(8,128)S(1)} %get-tuple-element.300, s32[17]{0:T(128)S(1)} %get-tuple-element.314), kind=kCustom, calls=%fused_computation.1 | custom fusion | bytes 6684876 | tf_op jit(solution)/shard_map/vmap()/gather | solution.py:92
  116.1 2.7 %gather_fusion = f32[17,16,24,128]{3,2,1,0:T(8,128)} fusion(f32[32,24,128]{2,1,0:T(8,128)S(1)} %get-tuple-element.301, s32[17]{0:T(128)S(1)} %get-tuple-element.315), kind=kCustom, calls=%fused_computation | custom fusion | bytes 6684876 | tf_op jit(solution)/shard_map/vmap()/gather | solution.py:91
  118.8 4.5 %multiply_convert_fusion = bf16[17,16,24,128]{3,2,1,0:T(8,128)(2,1)} fusion(f32[17,16,24,128]{3,2,1,0:T(8,128)} %gather_fusion, f32[17,16,24,128]{3,2,1,0:T(8,128)} %gather_fusion.1), kind=kLoop, calls=%fused_computation.6 | loop fusion | flops 1671168 | bytes 8355840 | tf_op jit(solution)/shard_map/vmap()/convert_element_type | solution.py:93
  123.4 0.8 fusion.56
  (104 shorter events, 20.6 us)
Async XLA Ops:
  0.6 17.1 %copy-start.5 = (s32[4]{0:T(128)S(1)}, s32[4]{0:T(128)}, u32[]{:S(2)}) copy-start(s32[4]{0:T(128)} %constant.274.clone.1) | copy-start | bytes 52
  0.6 19.1 %copy-start.1 = (f32[16,24,128]{2,1,0:T(8,128)S(1)}, f32[16,24,128]{2,1,0:T(8,128)}, u32[]{:S(2)}) copy-start(f32[16,24,128]{2,1,0:T(8,128)} %param.34) | copy-start | bytes 589828
  0.7 19.1 %copy-start = (f32[16,24,128]{2,1,0:T(8,128)S(1)}, f32[16,24,128]{2,1,0:T(8,128)}, u32[]{:S(2)}) copy-start(f32[16,24,128]{2,1,0:T(8,128)} %param.32) | copy-start | bytes 589828
  0.7 16.6 %copy-start.6 = (s32[16]{0:T(128)S(1)}, s32[16]{0:T(128)}, u32[]{:S(2)}) copy-start(s32[16]{0:T(128)} %param.36) | copy-start | bytes 196
  1.6 18.1 %collective-permute-start.1 = (f32[2,4,24,128]{3,2,1,0:T(8,128)S(1)}, f32[2,4,24,128]{3,2,1,0:T(8,128)S(1)}, u32[]{:S(2)}, u32[]{:S(2)}) collective-permute-start(f32[2,4,24,128]{3,2,1,0:T(8,128)S(1)} %get-tuple-element.308), channel_id=1, source_target_pairs={{0,1},{1,2},{2,3},{3,4},{4,5},{5,6},{6,7},{7,8},{8,9},{9,10},{10,1... | collective-permute-start | bytes 294920 | tf_op jit(solution)/shard_map/ppermute | solution.py:23
  3.6 16.2 %collective-permute-start = (f32[2,4,24,128]{3,2,1,0:T(8,128)S(1)}, f32[2,4,24,128]{3,2,1,0:T(8,128)S(1)}, u32[]{:S(2)}, u32[]{:S(2)}) collective-permute-start(f32[2,4,24,128]{3,2,1,0:T(8,128)S(1)} %get-tuple-element.309), channel_id=1, source_target_pairs={{1,0},{2,1},{3,2},{4,3},{5,4},{6,5},{7,6},{8,7},{9,8},{10,9},{11,1... | collective-permute-start | bytes 294920 | tf_op jit(solution)/shard_map/ppermute | solution.py:24
  12.0 5.3 %copy-start.9 = (s32[16]{0:T(128)}, s32[16]{0:T(128)S(1)}, u32[]{:S(2)}) copy-start(s32[16]{0:T(128)S(1)} %broadcast_subtract_fusion.1) | copy-start | bytes 196
  19.7 0.9 copy-start.2
  19.7 1.0 copy-start.3
  19.7 1.1 copy-start.4
  22.4 10.5 %copy-start.10 = (s32[16]{0:T(128)S(1)}, s32[16]{0:T(128)}, u32[]{:S(2)}) copy-start(s32[16]{0:T(128)} %copy-done.9) | copy-start | bytes 196
  28.5 4.8 %collective-permute-start.2 = (f32[2,4,24,128]{3,2,1,0:T(8,128)S(1)}, f32[2,4,24,128]{3,2,1,0:T(8,128)S(1)}, u32[]{:S(2)}, u32[]{:S(2)}) collective-permute-start(f32[2,4,24,128]{3,2,1,0:T(8,128)S(1)} %get-tuple-element.304), channel_id=1, source_target_pairs={{1,0},{2,1},{3,2},{4,3},{5,4},{6,5},{7,6},{8,7},{9,8},{10,9},{11,1... | collective-permute-start | bytes 294920 | tf_op jit(solution)/shard_map/ppermute | solution.py:24
  30.5 6.8 %collective-permute-start.3 = (f32[2,4,24,128]{3,2,1,0:T(8,128)S(1)}, f32[2,4,24,128]{3,2,1,0:T(8,128)S(1)}, u32[]{:S(2)}, u32[]{:S(2)}) collective-permute-start(f32[2,4,24,128]{3,2,1,0:T(8,128)S(1)} %get-tuple-element.305), channel_id=1, source_target_pairs={{0,1},{1,2},{2,3},{3,4},{4,5},{5,6},{6,7},{7,8},{8,9},{9,10},{10,1... | collective-permute-start | bytes 294920 | tf_op jit(solution)/shard_map/ppermute | solution.py:23
  45.6 7.4 %copy-start.7 = (s32[17]{0:T(128)S(1)}, s32[17]{0:T(128)}, u32[]{:S(2)}) copy-start(s32[17]{0:T(128)} %param.41) | copy-start | bytes 208
  45.6 7.4 %copy-start.8 = (f32[17]{0:T(128)S(1)}, f32[17]{0:T(128)}, u32[]{:S(2)}) copy-start(f32[17]{0:T(128)} %convert_multiply_fusion) | copy-start | bytes 208
  46.4 65.9 %collective-permute-start.4 = (f32[2,8,24,128]{3,2,1,0:T(8,128)}, f32[2,8,24,128]{3,2,1,0:T(8,128)}, u32[]{:S(2)}, u32[]{:S(2)}) collective-permute-start(f32[2,8,24,128]{3,2,1,0:T(8,128)} %get-tuple-element.302), channel_id=1, source_target_pairs={{0,1},{1,2},{2,3},{3,4},{4,5},{5,6},{6,7},{7,8},{8,9},{9,10},{10,1... | collective-permute-start | bytes 589832 | tf_op jit(solution)/shard_map/ppermute | solution.py:23
  48.3 64.0 %collective-permute-start.5 = (f32[2,8,24,128]{3,2,1,0:T(8,128)}, f32[2,8,24,128]{3,2,1,0:T(8,128)}, u32[]{:S(2)}, u32[]{:S(2)}) collective-permute-start(f32[2,8,24,128]{3,2,1,0:T(8,128)} %get-tuple-element.303), channel_id=1, source_target_pairs={{1,0},{2,1},{3,2},{4,3},{5,4},{6,5},{7,6},{8,7},{9,8},{10,9},{11,1... | collective-permute-start | bytes 589832 | tf_op jit(solution)/shard_map/ppermute | solution.py:24
  105.8 17.5 %collective-permute-start.6 = (f32[2,16,24,128]{3,2,1,0:T(8,128)}, f32[2,16,24,128]{3,2,1,0:T(8,128)S(1)}, u32[]{:S(2)}, u32[]{:S(2)}) collective-permute-start(f32[2,16,24,128]{3,2,1,0:T(8,128)} %get-tuple-element.296), channel_id=1, source_target_pairs={{0,1},{1,2},{2,3},{3,4},{4,5},{5,6},{6,7},{7,8},{8,9},{9,10},{10,1... | collective-permute-start | bytes 1179656 | tf_op jit(solution)/shard_map/ppermute | solution.py:32
  107.7 15.6 %collective-permute-start.7 = (f32[2,16,24,128]{3,2,1,0:T(8,128)S(1)}, f32[2,16,24,128]{3,2,1,0:T(8,128)S(1)}, u32[]{:S(2)}, u32[]{:S(2)}) collective-permute-start(f32[2,16,24,128]{3,2,1,0:T(8,128)S(1)} %get-tuple-element.297), channel_id=1, source_target_pairs={{1,0},{2,1},{3,2},{4,3},{5,4},{6,5},{7,6},{8,7},{9,8},{10,9},{11,1... | collective-permute-start | bytes 1179656 | tf_op jit(solution)/shard_map/ppermute | solution.py:32
where the time goes:
time: 125 us; the launch traced here: 124 us
  local copies, waits for them, and re-layouts  42.3 us (34%)
  other arithmetic  37.4 us (30%)
  starting transfers between devices  23.7 us (19%)
  loops' own time  11.9 us (10%)
  waiting for transfers between devices  3.98 us (3%)
  matrix products  3.93 us (3%)
    add x17, other arithmetic, accumulate(): return carry + weights[index] * jnp.stack([from_record, from_source])  16.1 us
    another operation x1, loops' own time, accumulate_terms(): return lax.fori_loop(0, NLAG, accumulate, empty)  11.9 us
    ppermute x3, starting transfers between devices, extended(): after = lax.ppermute(first, axis, down)  11 us
    dynamic_slice x17, local copies, waits for them, and re-layouts, accumulate(): return carry + weights[index] * jnp.stack([from_record, from_source])  10.4 us
    dynamic_slice x17, local copies, waits for them, and re-layouts, accumulate(): shift_cells = offsets[index]  9.9 us
    ppermute x2, starting transfers between devices, from_behind(): return lax.ppermute(block, axis, route)  6.45 us
    ppermute x3, starting transfers between devices, extended(): before = lax.ppermute(last, axis, up)  6.24 us
    another operation x4, other arithmetic  6.12 us
  transfers between devices with their start and end apart: 8, of which 1 were waited for; matrix products, arithmetic and copies ran while one was open for 52% of the time, Pallas kernels for 0%

commit v1 on v0

v1 whole, which is shorter than its diff:
```python
import functools

import jax
import jax.numpy as jnp
from jax import lax
from jax.experimental import pallas as pl
from jax.experimental.pallas import tpu as pltpu
from jax.sharding import PartitionSpec as P

STEPS = 2
LAG_MAX = 8
REACH = 4
PAD = 8

stencil = (-205.0 / 72.0, 8.0 / 5.0, -1.0 / 5.0, 8.0 / 315.0, -1.0 / 560.0)
source_depth = 3
record_depth = 1

VMEM = pl.BlockSpec(memory_space=pltpu.VMEM)
SMEM = pl.BlockSpec(memory_space=pltpu.SMEM)
ANY = pl.BlockSpec(memory_space=pl.ANY)


def params(mib):
    return pltpu.CompilerParams(vmem_limit_bytes=mib << 20)


def pack_kernel(ve, sp, sn, rp, rn, near, far, sems):
    extent = ve.shape[0]
    odd = lax.rem(lax.axis_index("gx"), 2)
    copies = []
    for out, right in ((near, 1 - odd), (far, odd)):
        at = 0
        for field, width in ((sn, 2 * REACH), (rn, 2 * REACH), (sp, REACH), (rp, REACH), (ve, REACH)):
            first = right * (extent - width)
            copies.append(
                pltpu.make_async_copy(
                    field.at[pl.ds(first, width)],
                    out.at[pl.ds(at, width)],
                    sems.at[len(copies)],
                )
            )
            at += width
    for c in copies:
        c.start()
    for c in copies:
        c.wait()


def shifted(u, k, lane):
    cells_z = u.shape[-1]
    rolled = pltpu.roll(u, k % cells_z, u.ndim - 1)
    inside = lane >= k if k > 0 else lane < cells_z + k
    return jnp.where(inside, rolled, 0.0)


def laplace_plane(u_ref, f, x, cells_y, lane):
    mid = u_ref[f, x, PAD : PAD + cells_y, :]
    total = 3.0 * stencil[0] * mid
    for k in range(1, 5):
        beside = u_ref[f, x + k, PAD : PAD + cells_y, :] + u_ref[f, x - k, PAD : PAD + cells_y, :]
        beside = beside + u_ref[f, x, PAD + k : PAD + k + cells_y, :]
        beside = beside + u_ref[f, x, PAD - k : PAD - k + cells_y, :]
        beside = beside + shifted(mid, k, lane)
        beside = beside + shifted(mid, -k, lane)
        total = total + stencil[k] * beside
    return mid, total


def source_plane(place_x, place_y, amplitude, first, cells_y):
    count = place_x.shape[1]
    row = lax.broadcasted_iota(jnp.int32, (128, count), 0)
    hit = (place_x - first) == lax.rem(row, 64)
    amp = jnp.where(row < 64, amplitude[0:1, :], amplitude[1:2, :])
    amp = jnp.where(hit, amp, 0.0)
    hit_y = (place_y == lax.broadcasted_iota(jnp.int32, (cells_y, count), 0)).astype(jnp.float32)
    return lax.dot_general(
        hit_y,
        amp,
        (((1,), (1,)), ((), ())),
        precision=lax.Precision.HIGHEST,
        preferred_element_type=jnp.float32,
    )


def step_kernel(
    ve, sp, sn, rp, rn, near, far, s_x, s_y, s_a, r_x, r_y, r_a, out, now, nxt, pri, vel, inj
):
    extent, cells_y, cells_z = ve.shape
    index = lax.axis_index("gx")
    odd = lax.rem(index, 2)
    first = index * extent - REACH
    lane = lax.broadcasted_iota(jnp.int32, (cells_y, cells_z), 1)
    inj[0] = source_plane(s_x[...], s_y[...], s_a[...], first, cells_y)
    inj[1] = source_plane(r_x[...], r_y[...], r_a[...], first, cells_y)

    rim = jnp.zeros((2, now.shape[1], PAD, cells_z), jnp.float32)
    now[:, :, 0:PAD, :] = rim
    now[:, :, PAD + cells_y :, :] = rim
    nxt[:, :, 0:PAD, :] = rim[:, : nxt.shape[1]]
    nxt[:, :, PAD + cells_y :, :] = rim[:, : nxt.shape[1]]
    mid_y = slice(PAD, PAD + cells_y)
    w = 2 * REACH
    now[0, w : w + extent, mid_y, :] = sn[...]
    now[1, w : w + extent, mid_y, :] = rn[...]
    pri[0, REACH : REACH + extent] = sp[...]
    pri[1, REACH : REACH + extent] = rp[...]
    vel[REACH : REACH + extent] = ve[...]

    def sides(left, right):
        for at, got in ((0, left), (1, right)):
            a = at * (w + extent)
            now[0, a : a + w, mid_y, :] = got[0:w]
            now[1, a : a + w, mid_y, :] = got[w : 2 * w]
            b = at * (REACH + extent)
            pri[0, b : b + REACH] = got[2 * w : 2 * w + REACH]
            pri[1, b : b + REACH] = got[2 * w + REACH : 3 * w]
            vel[b : b + REACH] = got[3 * w : 3 * w + REACH]

    @pl.when(odd == 0)
    def _():
        sides(far, near)

    @pl.when(odd == 1)
    def _():
        sides(near, far)

    def inject(f, t, i):
        depth = (source_depth, record_depth)[f]
        at = lax.rem(depth - (64 * t + i) + 256, 128)
        return jnp.where(lane == depth, pltpu.roll(inj[f], at, 1), 0.0)

    def first_step(i, carry):
        for f in range(2):
            mid, lap = laplace_plane(now, f, i + REACH, cells_y, lane)
            nxt[f, i, mid_y, :] = 2.0 * mid - pri[f, i] + vel[i] * lap + inject(f, 0, i)
        return carry

    lax.fori_loop(0, extent + 2 * REACH, first_step, 0)

    def second_step(i, carry):
        for f in range(2):
            mid, lap = laplace_plane(nxt, f, i + REACH, cells_y, lane)
            before = now[f, i + w, mid_y, :]
            out[f, i] = 2.0 * mid - before + vel[i + REACH] * lap + inject(f, 1, i + REACH)
        return carry

    lax.fori_loop(0, extent, second_step, 0)


def image_kernel(offsets, own, near, far, images, adj_s, adj_r, wide, squares, block, sems):
    extent = own.shape[1]
    count = images.shape[0]
    odd = lax.rem(lax.axis_index("gx"), 2)

    def fill(at, got):
        for f in range(2):
            v = got[f]
            wide[f, at : at + extent] = v
            squares[f, at : at + extent] = v * v

    fill(extent, own)

    @pl.when(odd == 0)
    def _():
        fill(0, far)
        fill(2 * extent, near)

    @pl.when(odd == 1)
    def _():
        fill(0, near)
        fill(2 * extent, far)

    def out_copy(k):
        return pltpu.make_async_copy(block.at[k], images.at[k], sems.at[k])

    def one_image(k, carry):
        shift = offsets[k]
        left = wide[0, pl.ds(extent - shift, extent)]
        right = wide[1, pl.ds(extent + shift, extent)]
        block[k] = (left * right).astype(jnp.bfloat16)
        out_copy(k).start()
        return carry

    lax.fori_loop(0, count, one_image, 0)

    def one_layer(i, carry):
        to_s = jnp.zeros(own.shape[2:], jnp.float32)
        to_r = jnp.zeros(own.shape[2:], jnp.float32)
        for k in range(count):
            shift = offsets[k]
            weight = (shift * shift).astype(jnp.float32) * (1.0 / (LAG_MAX * LAG_MAX * count))
            to_s = to_s + weight * squares[1, extent + i + 2 * shift]
            to_r = to_r + weight * squares[0, extent + i - 2 * shift]
        adj_s[i] = wide[0, extent + i] * to_s
        adj_r[i] = wide[1, extent + i] * to_r
        return carry

    lax.fori_loop(0, extent, one_layer, 0)

    def drain(k, carry):
        out_copy(k).wait()
        return carry

    lax.fori_loop(0, count, drain, 0)


def pairs(count):
    near = [(i, i ^ 1) for i in range(count)]
    far = [(i, i + 1 if i % 2 else i - 1) for i in range(count)]
    return near, [(a, b) for a, b in far if 0 <= b < count]


def per_device(
    velocity,
    source_prior,
    source_now,
    record_prior,
    record_now,
    source_inline,
    source_crossline,
    source_pulse,
    receiver_inline,
    receiver_crossline,
    receiver_trace,
    offsets,
):
    extent, cells_y, cells_z = velocity.shape
    near_pairs, far_pairs = pairs(lax.axis_size("gx"))
    fields = (velocity, source_prior, source_now, record_prior, record_now)
    f32 = functools.partial(jax.ShapeDtypeStruct, dtype=jnp.float32)
    edge = f32((7 * REACH, cells_y, cells_z))
    near, far = pl.pallas_call(
        pack_kernel,
        out_shape=(edge, edge),
        in_specs=[ANY] * 5,
        out_specs=(VMEM, VMEM),
        scratch_shapes=[pltpu.SemaphoreType.DMA((10,))],
        compiler_params=params(8),
    )(*fields)
    got_far = lax.ppermute(far, "gx", far_pairs)
    got_near = lax.ppermute(near, "gx", near_pairs)
    whole_y = cells_y + 2 * PAD
    final = pl.pallas_call(
        step_kernel,
        out_shape=f32((2, extent, cells_y, cells_z)),
        in_specs=[VMEM] * 13,
        out_specs=VMEM,
        scratch_shapes=[
            pltpu.VMEM((2, extent + 4 * REACH, whole_y, cells_z), jnp.float32),
            pltpu.VMEM((2, extent + 2 * REACH, whole_y, cells_z), jnp.float32),
            pltpu.VMEM((2, extent + 2 * REACH, cells_y, cells_z), jnp.float32),
            pltpu.VMEM((extent + 2 * REACH, cells_y, cells_z), jnp.float32),
            pltpu.VMEM((2, cells_y, cells_z), jnp.float32),
        ],
        compiler_params=params(16),
    )(
        *fields,
        got_near,
        got_far,
        source_inline[None, :],
        source_crossline[None, :],
        source_pulse.T,
        receiver_inline[None, :],
        receiver_crossline[None, :],
        receiver_trace.T,
    )
    final_far = lax.ppermute(final, "gx", far_pairs)
    final_near = lax.ppermute(final, "gx", near_pairs)
    count = offsets.shape[0]
    plane = f32((extent, cells_y, cells_z))
    return pl.pallas_call(
        image_kernel,
        out_shape=(
            jax.ShapeDtypeStruct((count, extent, cells_y, cells_z), jnp.bfloat16),
            plane,
            plane,
        ),
        in_specs=[SMEM, VMEM, VMEM, VMEM],
        out_specs=(ANY, VMEM, VMEM),
        scratch_shapes=[
            pltpu.VMEM((2, 3 * extent, cells_y, cells_z), jnp.float32),
            pltpu.VMEM((2, 3 * extent, cells_y, cells_z), jnp.float32),
            pltpu.VMEM((count, extent, cells_y, cells_z), jnp.bfloat16),
            pltpu.SemaphoreType.DMA((count,)),
        ],
        compiler_params=params(16),
    )(offsets, final, final_near, final_far)


def solution(mesh):
    in_specs = (
        P("gx", None, None),
        P(("shots", "gx"), None, None),
        P(("shots", "gx"), None, None),
        P(("shots", "gx"), None, None),
        P(("shots", "gx"), None, None),
        P("shots"),
        P("shots"),
        P("shots", None),
        P("shots"),
        P("shots"),
        P("shots", None),
        P(),
    )
    out_specs = (
        P("shots", "gx", None, None),
        P(("shots", "gx"), None, None),
        P(("shots", "gx"), None, None),
    )
    return jax.shard_map(
        per_device, mesh=mesh, in_specs=in_specs, out_specs=out_specs, check_vma=False
    )
```

time: 125 us -> 49.2 us (0.39)
  the two profiles are of different devices: /device:TPU:10 before, /device:TPU:1 now
where the time goes in v1:
time: 49.2 us; the launch traced here: 48.7 us
  waiting for transfers between devices  15.6 us (32%)
  local copies, waits for them, and re-layouts  13.3 us (27%)
  Pallas kernels  10.1 us (21%)
  starting transfers between devices  9.03 us (18%)
  between operations  0.7 us (1%)
    unnamed x34, local copies, waits for them, and re-layouts  13.3 us
    ppermute x1, waiting for transfers between devices, per_device(): got_far = lax.ppermute(far, 'gx', far_pairs)  7.85 us
    ppermute x1, waiting for transfers between devices, per_device(): final_far = lax.ppermute(final, 'gx', far_pairs)  7.75 us
    pallas_call x1, Pallas kernels, per_device(): pl.pallas_call(step_kernel, out_shape=f32((2, extent, cells_y, cells_z)),...  5.9 us
    ppermute x1, starting transfers between devices, per_device(): got_far = lax.ppermute(far, 'gx', far_pairs)  4.52 us
    ppermute x1, starting transfers between devices, per_device(): final_far = lax.ppermute(final, 'gx', far_pairs)  4.35 us
    pallas_call x1, Pallas kernels, per_device(): pl.pallas_call(image_kernel, out_shape=(jax.ShapeDtypeStruct((count, exte...  3.19 us
  transfers between devices with their start and end apart: 4, of which 2 were waited for; matrix products, arithmetic and copies ran while one was open for 0% of the time, Pallas kernels for 0%

profile of v1, /device:TPU:1, one launch (start us, length us, event | category | flops | bytes accessed | tf_op | source)
XLA Modules:
  0.0 48.7 jit_solution(15797449838074423407)
XLA Ops:
  0.6 0.0 copy-start
  0.6 0.9 %copy-done = f32[16,24,128]{2,1,0:T(8,128)S(1)} copy-done((f32[16,24,128]{2,1,0:T(8,128)S(1)}, f32[16,24,128]{2,1,0:T(8,128)}, u32[]{:S(2)}) %copy-start) | copy-done | bytes 196632
  1.6 0.0 copy-start.2
  1.6 0.9 %copy-done.2 = f32[16,24,128]{2,1,0:T(8,128)S(1)} copy-done((f32[16,24,128]{2,1,0:T(8,128)S(1)}, f32[16,24,128]{2,1,0:T(8,128)}, u32[]{:S(2)}) %copy-start.2) | copy-done | bytes 196632
  2.5 0.0 copy-start.4
  2.5 0.9 %copy-done.4 = f32[16,24,128]{2,1,0:T(8,128)S(1)} copy-done((f32[16,24,128]{2,1,0:T(8,128)S(1)}, f32[16,24,128]{2,1,0:T(8,128)}, u32[]{:S(2)}) %copy-start.4) | copy-done | bytes 196632
  3.4 0.0 copy-start.6
  3.4 0.9 %copy-done.6 = f32[16,24,128]{2,1,0:T(8,128)S(1)} copy-done((f32[16,24,128]{2,1,0:T(8,128)S(1)}, f32[16,24,128]{2,1,0:T(8,128)}, u32[]{:S(2)}) %copy-start.6) | copy-done | bytes 196632
  4.3 0.0 copy-start.8
  4.3 0.9 %copy-done.8 = f32[16,24,128]{2,1,0:T(8,128)S(1)} copy-done((f32[16,24,128]{2,1,0:T(8,128)S(1)}, f32[16,24,128]{2,1,0:T(8,128)}, u32[]{:S(2)}) %copy-start.8) | copy-done | bytes 196632
  5.3 0.0 copy-start.16
  5.3 1.0 %shard_map.139 = (f32[28,24,128]{2,1,0:T(8,128)S(1)}, f32[28,24,128]{2,1,0:T(8,128)S(1)}) custom-call(f32[16,24,128]{2,1,0:T(8,128)S(1)} %copy-done, f32[16,24,128]{2,1,0:T(8,128)S(1)} %copy-done.2, f32[16,24,128]{2,1,0:T(8,128)S(1)} %copy-done.4, f32[16,24,128]{2,1,0:T(8,128)S(1)} %copy-done.6, f32[16,24,128]{2,1,0:T(8,128)S(1)} %copy-done.8), custom_call_target="tpu_custom_call" | custom-call | tf_op jit(solution)/shard_map/pallas_call | solution.py:233
  6.2 0.1 collective-permute-start
  6.3 4.5 %collective-permute-start.1 = (f32[28,24,128]{2,1,0:T(8,128)S(1)}, f32[28,24,128]{2,1,0:T(8,128)S(1)}, u32[]{:S(2)}, u32[]{:S(2)}) collective-permute-start(f32[28,24,128]{2,1,0:T(8,128)S(1)} %get-tuple-element.6), channel_id=1, source_target_pairs={{1,2},{2,1},{3,4},{4,3},{5,6},{6,5},{7,8},{8,7},{9,10},{10,9},{11,... | collective-permute-start | bytes 1032200 | tf_op jit(solution)/shard_map/ppermute | solution.py:241
  10.9 0.0 collective-permute-done.near
  10.9 7.8 %collective-permute-done.1.far = f32[28,24,128]{2,1,0:T(8,128)S(1)} collective-permute-done((f32[28,24,128]{2,1,0:T(8,128)S(1)}, f32[28,24,128]{2,1,0:T(8,128)S(1)}, u32[]{:S(2)}, u32[]{:S(2)}) %collective-permute-start.1) | collective-permute-done | bytes 344096 | tf_op jit(solution)/shard_map/ppermute | solution.py:241
  18.7 0.0 copy-start.1
  18.7 0.9 %copy-done.1 = f32[16,24,128]{2,1,0:T(8,128)S(1)} copy-done((f32[16,24,128]{2,1,0:T(8,128)S(1)}, f32[16,24,128]{2,1,0:T(8,128)}, u32[]{:S(2)}) %copy-start.1) | copy-done | bytes 196632
  19.6 0.0 copy-start.3
  19.7 0.9 %copy-done.3 = f32[16,24,128]{2,1,0:T(8,128)S(1)} copy-done((f32[16,24,128]{2,1,0:T(8,128)S(1)}, f32[16,24,128]{2,1,0:T(8,128)}, u32[]{:S(2)}) %copy-start.3) | copy-done | bytes 196632
  20.6 0.0 copy-start.5
  20.6 0.9 %copy-done.5 = f32[16,24,128]{2,1,0:T(8,128)S(1)} copy-done((f32[16,24,128]{2,1,0:T(8,128)S(1)}, f32[16,24,128]{2,1,0:T(8,128)}, u32[]{:S(2)}) %copy-start.5) | copy-done | bytes 196632
  21.5 0.0 copy-start.7
  21.5 0.9 %copy-done.7 = f32[16,24,128]{2,1,0:T(8,128)S(1)} copy-done((f32[16,24,128]{2,1,0:T(8,128)S(1)}, f32[16,24,128]{2,1,0:T(8,128)}, u32[]{:S(2)}) %copy-start.7) | copy-done | bytes 196632
  22.4 0.0 copy-start.9
  22.4 0.9 %copy-done.9 = f32[16,24,128]{2,1,0:T(8,128)S(1)} copy-done((f32[16,24,128]{2,1,0:T(8,128)S(1)}, f32[16,24,128]{2,1,0:T(8,128)}, u32[]{:S(2)}) %copy-start.9) | copy-done | bytes 196632
  23.4 0.0 copy-start.10
  23.4 0.7 %copy-done.10 = f32[1024,2]{0,1:T(2,128)S(1)} copy-done((f32[1024,2]{0,1:T(2,128)S(1)}, f32[1024,2]{0,1:T(2,128)}, u32[]{:S(2)}) %copy-start.10) | copy-done | bytes 8216
  24.1 0.0 copy-start.11
  24.1 0.7 %copy-done.11 = s32[1024]{0:T(1024)S(1)} copy-done((s32[1024]{0:T(1024)S(1)}, s32[1024]{0:T(1024)}, u32[]{:S(2)}) %copy-start.11) | copy-done | bytes 4120
  24.7 0.0 copy-start.12
  24.7 0.7 %copy-done.12 = s32[1024]{0:T(1024)S(1)} copy-done((s32[1024]{0:T(1024)S(1)}, s32[1024]{0:T(1024)}, u32[]{:S(2)}) %copy-start.12) | copy-done | bytes 4120
  25.4 0.0 copy-start.13
  25.4 0.7 %copy-done.13 = f32[16,2]{0,1:T(2,128)S(1)} copy-done((f32[16,2]{0,1:T(2,128)S(1)}, f32[16,2]{0,1:T(2,128)}, u32[]{:S(2)}) %copy-start.13) | copy-done | bytes 152
  26.1 0.0 copy-start.14
  26.1 0.7 %copy-done.14 = s32[16]{0:T(128)S(1)} copy-done((s32[16]{0:T(128)S(1)}, s32[16]{0:T(128)}, u32[]{:S(2)}) %copy-start.14) | copy-done | bytes 88
  26.8 0.0 copy-start.15
  26.8 0.7 %copy-done.15 = s32[16]{0:T(128)S(1)} copy-done((s32[16]{0:T(128)S(1)}, s32[16]{0:T(128)}, u32[]{:S(2)}) %copy-start.15) | copy-done | bytes 88
  27.4 5.9 %shard_map.140.own = f32[2,16,24,128]{3,2,1,0:T(8,128)S(1)} custom-call(f32[16,24,128]{2,1,0:T(8,128)S(1)} %copy-done.1, f32[16,24,128]{2,1,0:T(8,128)S(1)} %copy-done.3, f32[16,24,128]{2,1,0:T(8,128)S(1)} %copy-done.5, f32[16,24,128]{2,1,0:T(8,128)S(1)} %copy-done.7, f32[16,24,128]{2,1,0:T(8,128)S(1)} %copy-done.9, ...), custom_call_target="tpu_custom_call" | custom-call | tf_op jit(solution)/shard_map/pallas_call | solution.py:244
  33.3 4.3 %collective-permute-start.3 = (f32[2,16,24,128]{3,2,1,0:T(8,128)S(1)}, f32[2,16,24,128]{3,2,1,0:T(8,128)S(1)}, u32[]{:S(2)}, u32[]{:S(2)}) collective-permute-start(f32[2,16,24,128]{3,2,1,0:T(8,128)S(1)} %shard_map.140.own), channel_id=1, source_target_pairs={{1,2},{2,1},{3,4},{4,3},{5,6},{6,5},{7,8},{8,7},{9,10},{10,9},{11,... | collective-permute-start | bytes 1179656 | tf_op jit(solution)/shard_map/ppermute | solution.py:268
  37.7 0.1 collective-permute-start.2
  37.8 7.7 %collective-permute-done.3.far = f32[2,16,24,128]{3,2,1,0:T(8,128)S(1)} collective-permute-done((f32[2,16,24,128]{3,2,1,0:T(8,128)S(1)}, f32[2,16,24,128]{3,2,1,0:T(8,128)S(1)}, u32[]{:S(2)}, u32[]{:S(2)}) %collective-permute-start.3) | collective-permute-done | bytes 393248 | tf_op jit(solution)/shard_map/ppermute | solution.py:268
  45.5 0.0 collective-permute-done.2.near
  45.5 0.0 copy-done.16
  45.5 3.2 %shard_map.141 = (bf16[17,16,24,128]{3,2,1,0:T(8,128)(2,1)}, f32[16,24,128]{2,1,0:T(8,128)}, f32[16,24,128]{2,1,0:T(8,128)}) custom-call(s32[17]{0:T(128)S(1)} %copy-done.16, f32[2,16,24,128]{3,2,1,0:T(8,128)S(1)} %shard_map.140.own, f32[2,16,24,128]{3,2,1,0:T(8,128)S(1)} %collective-permute-done.2.near, f32[2,16,24,128]{3,2,1,0:T(8,128)S(1)} %collective-permute-done.3.far), custom_call_target="tpu_custom_call" | custom-call | tf_op jit(solution)/shard_map/pallas_call | solution.py:272
Async XLA Ops:
  0.6 0.9 %copy-start = (f32[16,24,128]{2,1,0:T(8,128)S(1)}, f32[16,24,128]{2,1,0:T(8,128)}, u32[]{:S(2)}) copy-start(f32[16,24,128]{2,1,0:T(8,128)} %ve.3) | copy-start | bytes 589828
  1.6 0.9 %copy-start.2 = (f32[16,24,128]{2,1,0:T(8,128)S(1)}, f32[16,24,128]{2,1,0:T(8,128)}, u32[]{:S(2)}) copy-start(f32[16,24,128]{2,1,0:T(8,128)} %sp.3) | copy-start | bytes 589828
  2.5 0.9 %copy-start.4 = (f32[16,24,128]{2,1,0:T(8,128)S(1)}, f32[16,24,128]{2,1,0:T(8,128)}, u32[]{:S(2)}) copy-start(f32[16,24,128]{2,1,0:T(8,128)} %sn.3) | copy-start | bytes 589828
  3.4 0.9 %copy-start.6 = (f32[16,24,128]{2,1,0:T(8,128)S(1)}, f32[16,24,128]{2,1,0:T(8,128)}, u32[]{:S(2)}) copy-start(f32[16,24,128]{2,1,0:T(8,128)} %rp.3) | copy-start | bytes 589828
  4.3 0.9 %copy-start.8 = (f32[16,24,128]{2,1,0:T(8,128)S(1)}, f32[16,24,128]{2,1,0:T(8,128)}, u32[]{:S(2)}) copy-start(f32[16,24,128]{2,1,0:T(8,128)} %rn.3) | copy-start | bytes 589828
  5.3 40.3 %copy-start.16 = (s32[17]{0:T(128)S(1)}, s32[17]{0:T(128)}, u32[]{:S(2)}) copy-start(s32[17]{0:T(128)} %offsets.1) | copy-start | bytes 208
  6.2 4.6 %collective-permute-start = (f32[28,24,128]{2,1,0:T(8,128)S(1)}, f32[28,24,128]{2,1,0:T(8,128)S(1)}, u32[]{:S(2)}, u32[]{:S(2)}) collective-permute-start(f32[28,24,128]{2,1,0:T(8,128)S(1)} %get-tuple-element.5), channel_id=1, source_target_pairs={{0,1},{1,0},{2,3},{3,2},{4,5},{5,4},{6,7},{7,6},{8,9},{9,8},{10,11... | collective-permute-start | bytes 1032200 | tf_op jit(solution)/shard_map/ppermute | solution.py:242
  6.3 12.4 %collective-permute-start.1 = (f32[28,24,128]{2,1,0:T(8,128)S(1)}, f32[28,24,128]{2,1,0:T(8,128)S(1)}, u32[]{:S(2)}, u32[]{:S(2)}) collective-permute-start(f32[28,24,128]{2,1,0:T(8,128)S(1)} %get-tuple-element.6), channel_id=1, source_target_pairs={{1,2},{2,1},{3,4},{4,3},{5,6},{6,5},{7,8},{8,7},{9,10},{10,9},{11,... | collective-permute-start | bytes 1032200 | tf_op jit(solution)/shard_map/ppermute | solution.py:241
  18.7 0.9 %copy-start.1 = (f32[16,24,128]{2,1,0:T(8,128)S(1)}, f32[16,24,128]{2,1,0:T(8,128)}, u32[]{:S(2)}) copy-start(f32[16,24,128]{2,1,0:T(8,128)} %ve.3) | copy-start | bytes 589828
  19.6 0.9 %copy-start.3 = (f32[16,24,128]{2,1,0:T(8,128)S(1)}, f32[16,24,128]{2,1,0:T(8,128)}, u32[]{:S(2)}) copy-start(f32[16,24,128]{2,1,0:T(8,128)} %sp.3) | copy-start | bytes 589828
  20.6 0.9 %copy-start.5 = (f32[16,24,128]{2,1,0:T(8,128)S(1)}, f32[16,24,128]{2,1,0:T(8,128)}, u32[]{:S(2)}) copy-start(f32[16,24,128]{2,1,0:T(8,128)} %sn.3) | copy-start | bytes 589828
  21.5 0.9 %copy-start.7 = (f32[16,24,128]{2,1,0:T(8,128)S(1)}, f32[16,24,128]{2,1,0:T(8,128)}, u32[]{:S(2)}) copy-start(f32[16,24,128]{2,1,0:T(8,128)} %rp.3) | copy-start | bytes 589828
  22.4 0.9 %copy-start.9 = (f32[16,24,128]{2,1,0:T(8,128)S(1)}, f32[16,24,128]{2,1,0:T(8,128)}, u32[]{:S(2)}) copy-start(f32[16,24,128]{2,1,0:T(8,128)} %rn.3) | copy-start | bytes 589828
  23.4 0.7 %copy-start.10 = (f32[1024,2]{0,1:T(2,128)S(1)}, f32[1024,2]{0,1:T(2,128)}, u32[]{:S(2)}) copy-start(f32[1024,2]{0,1:T(2,128)} %param.22) | copy-start | bytes 24580
  24.1 0.7 %copy-start.11 = (s32[1024]{0:T(1024)S(1)}, s32[1024]{0:T(1024)}, u32[]{:S(2)}) copy-start(s32[1024]{0:T(1024)} %param.20) | copy-start | bytes 12292
  24.7 0.7 %copy-start.12 = (s32[1024]{0:T(1024)S(1)}, s32[1024]{0:T(1024)}, u32[]{:S(2)}) copy-start(s32[1024]{0:T(1024)} %param.21) | copy-start | bytes 12292
  25.4 0.7 %copy-start.13 = (f32[16,2]{0,1:T(2,128)S(1)}, f32[16,2]{0,1:T(2,128)}, u32[]{:S(2)}) copy-start(f32[16,2]{0,1:T(2,128)} %param.19) | copy-start | bytes 388
  26.1 0.7 %copy-start.14 = (s32[16]{0:T(128)S(1)}, s32[16]{0:T(128)}, u32[]{:S(2)}) copy-start(s32[16]{0:T(128)} %param.17) | copy-start | bytes 196
  26.8 0.7 %copy-start.15 = (s32[16]{0:T(128)S(1)}, s32[16]{0:T(128)}, u32[]{:S(2)}) copy-start(s32[16]{0:T(128)} %param.18) | copy-start | bytes 196
  33.3 12.2 %collective-permute-start.3 = (f32[2,16,24,128]{3,2,1,0:T(8,128)S(1)}, f32[2,16,24,128]{3,2,1,0:T(8,128)S(1)}, u32[]{:S(2)}, u32[]{:S(2)}) collective-permute-start(f32[2,16,24,128]{3,2,1,0:T(8,128)S(1)} %shard_map.140.own), channel_id=1, source_target_pairs={{1,2},{2,1},{3,4},{4,3},{5,6},{6,5},{7,8},{8,7},{9,10},{10,9},{11,... | collective-permute-start | bytes 1179656 | tf_op jit(solution)/shard_map/ppermute | solution.py:268
  37.7 7.8 %collective-permute-start.2 = (f32[2,16,24,128]{3,2,1,0:T(8,128)S(1)}, f32[2,16,24,128]{3,2,1,0:T(8,128)S(1)}, u32[]{:S(2)}, u32[]{:S(2)}) collective-permute-start(f32[2,16,24,128]{3,2,1,0:T(8,128)S(1)} %shard_map.140.own), channel_id=1, source_target_pairs={{0,1},{1,0},{2,3},{3,2},{4,5},{5,4},{6,7},{7,6},{8,9},{9,8},{10,11... | collective-permute-start | bytes 1179656 | tf_op jit(solution)/shard_map/ppermute | solution.py:269
